TPU v7x, 256 devices: a whole 4x4x8 slice. The times are simulated.
256 devices in a mesh: dp: 64 (over z, y, core), mp: 4 (over x).
Axes of the slice: x: 4, y: 4, z: 8, core: 2. Of those that a mesh axis runs over, the one named last changes fastest.
Arguments:
- attention: bfloat16 [8192, 2048], P('dp', 'mp'), may hold values from -6 to 6
- residual: bfloat16 [8192, 2048], P('dp', 'mp'), may hold values from -6 to 6
- out_weight: bfloat16 [2048, 2048], P('mp', 'dp'), may hold values from -0.125 to 0.125
- ffn_gain: float32 [2048], P('mp'), may hold values from 0.1 to 1.9
- shared_gate: bfloat16 [2048, 2816], P('dp', 'mp'), may hold values from -0.125 to 0.125
- shared_up: bfloat16 [2048, 2816], P('dp', 'mp'), may hold values from -0.125 to 0.125
- shared_down: bfloat16 [2816, 2048], P('mp', 'dp'), may hold values from -0.109375 to 0.109375
- expert_gate: bfloat16 [64, 2048, 1408], P('dp', None, 'mp'), may hold values from -0.125 to 0.125
- expert_up: bfloat16 [64, 2048, 1408], P('dp', None, 'mp'), may hold values from -0.125 to 0.125
- expert_down: bfloat16 [64, 1408, 2048], P('dp', 'mp'), may hold values from -0.15625 to 0.15625
- route_ids: int32 [8192, 6], P('dp'), may hold values from 0 to 63, all different within a row; in each aligned block of 128 rows (0 to 127, 128 to 255, ...) at most 16 rows name the same one
- route_scores: float32 [8192, 6], P('dp'), may hold values from 0.05 to 1
- placement: int32 [64], replicated, may hold values from 0 to 63, each once
- next_gain: float32 [2048], P('mp'), may hold values from 0.1 to 1.9
Outputs:
- final: bfloat16 [8192, 2048], P('dp', 'mp')
- next_normed: bfloat16 [8192, 2048], P('dp', 'mp')
Inputs may be any that keep to these rules, and one draw needn't show every extreme that they name: `route_ids`: A token's 6 experts differ. In each aligned block of 128 rows (the rows of one index of dp) no expert is named by more than 16 rows, a bound that some block reaches. `placement`: each storage index is used by exactly one expert.
All inputs are finite; a program needn't handle non-finite values.
Results may differ from a plain program's by a relative error of at most 0.0075.
Values may be sent and summed in bfloat16 or wider, within the bound.
A program may use at most 128 MiB of HBM per device.

v0:
```python
import jax
import jax.numpy as jnp
from jax import lax
from jax.sharding import PartitionSpec as P

D = 2048
EPSILON = 1e-06


def matmul(left, right):
    return jnp.dot(left, right, preferred_element_type=jnp.float32)


def local(
    attention,
    residual,
    out_weight,
    ffn_gain,
    shared_gate,
    shared_up,
    shared_down,
    expert_gate,
    expert_up,
    expert_down,
    route_ids,
    route_scores,
    placement,
    next_gain,
):
    tok_rows = attention.shape[0]
    top_count = route_ids.shape[1]
    mp_count = lax.axis_size("mp")
    mp_index = lax.axis_index("mp")
    experts = lax.axis_size("dp")
    capacity = min(tok_rows, 8 * tok_rows // experts)
    model_width = D
    partial_value = matmul(attention, lax.all_gather(out_weight, "dp", axis=1, tiled=True))
    projected = lax.psum_scatter(partial_value, "mp", scatter_dimension=1, tiled=True)
    hidden = (residual.astype(jnp.float32) + projected).astype(jnp.bfloat16)
    hidden_float = hidden.astype(jnp.float32)
    squares = lax.psum(jnp.sum(hidden_float * hidden_float, axis=1), "mp")
    normed = (hidden_float * lax.rsqrt(squares / model_width + EPSILON)[:, None] * ffn_gain).astype(
        jnp.bfloat16
    )
    whole_rows = lax.all_gather(normed, "mp", axis=1, tiled=True)
    pieces = (
        lax.all_gather(shared_gate, "dp", axis=0, tiled=True),
        lax.all_gather(shared_up, "dp", axis=0, tiled=True),
    )
    shared_gval = matmul(whole_rows, pieces[0])
    shared_uval = matmul(whole_rows, pieces[1])
    shared_act = (jax.nn.silu(shared_gval) * shared_uval).astype(jnp.bfloat16)
    shared_part = matmul(shared_act, lax.all_gather(shared_down, "dp", axis=1, tiled=True))
    flat_ids = route_ids.reshape(-1)
    expert_iota = jnp.arange(experts, dtype=jnp.int32)
    one_hot = (flat_ids[:, None] == expert_iota[None, :]).astype(jnp.int32)
    target = jnp.sum(one_hot * placement[None, :], axis=1)
    slot = jnp.sum((jnp.cumsum(one_hot, axis=0) - one_hot) * one_hot, axis=1)
    token_of = jnp.arange(flat_ids.shape[0], dtype=jnp.int32) // top_count
    flat_scores = route_scores.reshape(-1)
    gate_local = expert_gate[0]
    up_local = expert_up[0]
    down_local = expert_down[0]
    quarter = capacity // mp_count
    owned = slot // quarter == mp_index
    position = jnp.where(owned, target * quarter + slot % quarter, experts * quarter)
    outgoing = (
        jnp.zeros((experts * quarter, model_width), jnp.bfloat16)
        .at[position]
        .set(whole_rows[token_of], mode="drop")
    )
    arrived = lax.all_to_all(
        outgoing.reshape(experts, quarter, model_width),
        "dp",
        split_axis=0,
        concat_axis=0,
        tiled=True,
    )
    in_rows = arrived.reshape(experts * quarter, model_width)
    pieces = (
        lax.all_gather(gate_local, "mp", axis=1, tiled=True),
        lax.all_gather(up_local, "mp", axis=1, tiled=True),
    )
    gate_val = matmul(in_rows, pieces[0])
    up_val = matmul(in_rows, pieces[1])
    activated = (jax.nn.silu(gate_val) * up_val).astype(jnp.bfloat16)
    outputs = matmul(activated, lax.all_gather(down_local, "mp", axis=0, tiled=True)).astype(
        jnp.bfloat16
    )
    returned = lax.all_to_all(
        outputs.reshape(experts, quarter, model_width),
        "dp",
        split_axis=0,
        concat_axis=0,
        tiled=True,
    )
    returned = returned.reshape(experts * quarter, model_width)
    bounded = jnp.minimum(position, experts * quarter - 1)
    weight = jnp.where(owned, flat_scores, 0.0)
    picked = returned[bounded].astype(jnp.float32) * weight[:, None]
    routed = jnp.sum(picked.reshape(tok_rows, top_count, model_width), axis=1)
    mixture = lax.psum_scatter(routed + shared_part, "mp", scatter_dimension=1, tiled=True)
    final = (hidden_float + mixture).astype(jnp.bfloat16)
    final_float = final.astype(jnp.float32)
    final_squares = lax.psum(jnp.sum(final_float * final_float, axis=1), "mp")
    next_normed = (
        final_float * lax.rsqrt(final_squares / model_width + EPSILON)[:, None] * next_gain
    ).astype(jnp.bfloat16)
    return (final, next_normed)


def solution(mesh):
    in_specs = (
        P("dp", "mp"),
        P("dp", "mp"),
        P("mp", "dp"),
        P("mp"),
        P("dp", "mp"),
        P("dp", "mp"),
        P("mp", "dp"),
        P("dp", None, "mp"),
        P("dp", None, "mp"),
        P("dp", "mp", None),
        P("dp", None),
        P("dp", None),
        P(),
        P("mp"),
    )
    out_specs = (P("dp", "mp"), P("dp", "mp"))
    return jax.shard_map(local, mesh=mesh, in_specs=in_specs, out_specs=out_specs, check_vma=False)
```

profile of v0, /device:TPU:8, one launch (start us, length us, event | category | flops | bytes accessed | tf_op | source)
XLA Modules:
  0.0 608.2 jit_solution(1089432544255874928)
XLA Ops:
  7.2 0.7 all-gather.11.cloned.1.call-update
  8.0 82.0 %all-gather.11.cloned.1.call-done = bf16[512,2048]{0,1:T(8,128)(2,1)} async-done(((bf16[512,32]{0,1:T(8,128)(2,1)}), bf16[512,2048]{0,1:T(8,128)(2,1)}) %all-gather.11.cloned.1.call-update) | async-done | bytes 2097168 | tf_op jit(solution)/shard_map/all_gather | solution.py:37
  90.0 3.4 fusion.50
  93.4 0.7 all-gather.19.cloned.1.call-update
  94.2 0.5 all-gather.21.cloned.1.call-update
  94.8 0.5 all-gather.23.cloned.1.call-update
  95.3 0.5 all-gather.13.cloned.1.call-update
  95.9 0.7 all-gather.15.cloned.1.call-update
  96.6 0.1 copy.24
  96.7 0.1 eq.55
  96.9 0.1 eq.51
  97.0 1.8 reduce-window.6
  98.8 0.3 slice_reduce_fusion
  99.2 0.1 fusion.36
  99.4 18.8 %reduce-scatter.3.cloned.1.call-done = f32[128,512]{1,0:T(8,128)} async-done(((f32[128,2048]{1,0:T(8,128)}), f32[128,512]{1,0:T(8,128)}) %reduce-scatter.3.cloned.1.call-update) | async-done | bytes 262160 | tf_op jit(solution)/shard_map/reduce_scatter | solution.py:38
  118.2 1.1 fusion.30
  119.3 8.5 %psum.14 = f32[128]{0:T(128)S(1)} all-reduce(f32[128]{0:T(128)S(1)} %get-tuple-element.8), channel_id=1, replica_groups=mesh['dp'=64,'mp'=4] {'mp'}, use_global_device_ids=true, to_apply=%region_6.7 | all-reduce | flops 128 | bytes 1024 | tf_op jit(solution)/shard_map/psum | solution.py:41
  127.8 0.1 fusion.32
  127.9 14.2 %all_gather.25 = bf16[128,2048]{1,0:T(8,128)(2,1)S(1)} all-gather(bf16[128,512]{1,0:T(8,128)(2,1)S(1)} %fusion.32), channel_id=1, replica_groups=mesh['dp'=64,'mp'=4] {'mp'}, dimensions={1}, use_global_device_ids=true | all-gather | bytes 655360 | tf_op jit(solution)/shard_map/all_gather | solution.py:45
  142.1 20.4 %scatter_custom_fusion = bf16[256,2048]{1,0:T(8,128)(2,1)S(1)} fusion(s32[768]{0:T(1024)S(1)} %get-tuple-element.5, bf16[128,2048]{1,0:T(8,128)(2,1)S(1)} %all_gather.25, s32[1024]{0:T(1024)S(1)} %pad_clamp_fusion.1, bf16[]{:T(256)} %constant.52.clone.1), kind=kCustom, calls=%fused_computation.10 | custom fusion | bytes 1048578 | tf_op jit(solution)/shard_map/scatter | solution.py:70
  162.5 1.3 reshape.214
  163.8 10.6 %all-to-all-start = ((bf16[64,4,2048]{2,1,0:T(4,128)(2,1)}), bf16[64,4,2048]{2,1,0:T(4,128)(2,1)S(1)}, u32[]{:S(2)}, u32[]{:S(2)}) async-start(bf16[64,4,2048]{2,1,0:T(4,128)(2,1)} %reshape.214), calls=%async_computation.1 | async-start | bytes 2097152 | tf_op jit(solution)/shard_map/all_to_all | solution.py:72
  174.4 0.7 all-gather.17.cloned.1.call-update
  175.1 28.0 %all-to-all-done = bf16[64,4,2048]{2,1,0:T(4,128)(2,1)S(1)} async-done(((bf16[64,4,2048]{2,1,0:T(4,128)(2,1)}), bf16[64,4,2048]{2,1,0:T(4,128)(2,1)S(1)}, u32[]{:S(2)}, u32[]{:S(2)}) %all-to-all-start) | async-done | bytes 1048608 | tf_op jit(solution)/shard_map/all_to_all | solution.py:72
  203.1 0.3 reshape.215
  203.4 5.6 fusion.4
  209.0 41.9 %all-gather.21.cloned.1.call-done = bf16[1,2048,1408]{1,2,0:T(8,128)(2,1)} async-done(((bf16[1,2048,352]{1,2,0:T(8,128)(2,1)}), bf16[1,2048,1408]{1,2,0:T(8,128)(2,1)}) %all-gather.21.cloned.1.call-update) | async-done | bytes 5767184 | tf_op jit(solution)/shard_map/all_gather | solution.py:82
  250.9 66.3 %all-gather.23.cloned.1.call-done = bf16[1,1408,2048]{2,1,0:T(8,128)(2,1)} async-done(((bf16[1,352,2048]{2,1,0:T(8,128)(2,1)}), bf16[1,1408,2048]{2,1,0:T(8,128)(2,1)}) %all-gather.23.cloned.1.call-update) | async-done | bytes 5767184 | tf_op jit(solution)/shard_map/all_gather | solution.py:87
  317.2 8.3 %fusion.14 = bf16[256,2048]{1,0:T(8,128)(2,1)S(1)} fusion(bf16[1,1408,2048]{2,1,0:T(8,128)(2,1)} %all-gather.23.cloned.1.call-done, bf16[256,2048]{1,0:T(8,128)(2,1)S(1)} %reshape.215, bf16[1,2048,1408]{1,2,0:T(8,128)(2,1)} %all-gather.21.cloned.1.call-done, f32[256,1408]{1,0:T(8,128)} %fusion.4), kind=kOutput, calls=%fused_computation.14 | convolution fusion | flops 2955476992 | bytes 15073280 | tf_op jit(solution)/shard_map/dot_general | solution.py:11
  325.5 1.2 reshape.216
  326.8 10.6 %all-to-all-start.1 = ((bf16[64,4,2048]{2,1,0:T(4,128)(2,1)}), bf16[64,4,2048]{2,1,0:T(4,128)(2,1)S(1)}, u32[]{:S(2)}, u32[]{:S(2)}) async-start(bf16[64,4,2048]{2,1,0:T(4,128)(2,1)} %reshape.216), calls=%async_computation.2 | async-start | bytes 2097152 | tf_op jit(solution)/shard_map/all_to_all | solution.py:90
  337.3 0.3 reduce-scatter.5.cloned.1.call-start
  337.6 0.1 reduce_sum.53
  337.7 0.1 copy.27
  337.8 0.1 copy.31
  338.0 63.4 %all-gather.13.cloned.1.call-done = bf16[2048,704]{1,0:T(8,128)(2,1)} async-done(((bf16[32,704]{1,0:T(8,128)(2,1)}), bf16[2048,704]{1,0:T(8,128)(2,1)}) %all-gather.13.cloned.1.call-update) | async-done | bytes 2883600 | tf_op jit(solution)/shard_map/all_gather | solution.py:47
  401.4 3.2 fusion.51
  404.6 0.3 reshape.217
  404.8 4.3 gather_fusion
  409.2 6.6 %reshape.218 = f32[128,6,2048]{2,1,0:T(8,128)} reshape(bf16[768,2048]{1,0:T(8,128)(2,1)} %gather_fusion) | data formatting | bytes 9437184 | tf_op jit(solution)/shard_map/convert_element_type | solution.py:100
  415.7 6.6 %multiply_reduce_fusion = f32[128,2048]{1,0:T(8,128)S(1)} fusion(f32[128,6,2048]{2,1,0:T(8,128)} %reshape.218, f32[128,6]{1,0:T(8,128)S(1)} %copy.31), kind=kLoop, calls=%fused_computation.3 | loop fusion | flops 2883584 | bytes 7343104 | tf_op jit(solution)/shard_map/reduce_sum | solution.py:101
  422.3 58.0 %all-gather.15.cloned.1.call-done = bf16[2048,704]{1,0:T(8,128)(2,1)} async-done(((bf16[32,704]{1,0:T(8,128)(2,1)}), bf16[2048,704]{1,0:T(8,128)(2,1)}) %all-gather.15.cloned.1.call-update) | async-done | bytes 2883600 | tf_op jit(solution)/shard_map/all_gather | solution.py:48
  480.3 78.9 %all-gather.17.cloned.1.call-done = bf16[704,2048]{0,1:T(8,128)(2,1)} async-done(((bf16[704,32]{0,1:T(8,128)(2,1)}), bf16[704,2048]{0,1:T(8,128)(2,1)}) %all-gather.17.cloned.1.call-update) | async-done | bytes 2883600 | tf_op jit(solution)/shard_map/all_gather | solution.py:53
  559.2 7.2 %convolution_add_fusion = f32[128,2048]{1,0:T(8,128)} fusion(f32[128,2048]{1,0:T(8,128)S(1)} %multiply_reduce_fusion, bf16[704,2048]{0,1:T(8,128)(2,1)} %all-gather.17.cloned.1.call-done, bf16[128,2048]{1,0:T(8,128)(2,1)S(1)} %all_gather.25, bf16[2048,704]{1,0:T(8,128)(2,1)} %all-gather.15.cloned.1.call-done, f32[128,704]{0,1:T(8,128)S(1)} %fusion.51), kind=kOutput, calls=%fused_computation.15 | convolution fusion | flops 739000320 | bytes 8749056 | tf_op jit(solution)/shard_map/dot_general | solution.py:11
  566.5 24.9 %reduce-scatter.5.cloned.1.call-done = f32[128,512]{1,0:T(8,128)} async-done(((f32[128,2048]{1,0:T(8,128)}), f32[128,512]{1,0:T(8,128)}) %reduce-scatter.5.cloned.1.call-update) | async-done | bytes 262160 | tf_op jit(solution)/shard_map/reduce_scatter | solution.py:102
  591.3 1.1 fusion.27
  592.4 8.5 %psum.15 = f32[128]{0:T(128)S(1)} all-reduce(f32[128]{0:T(128)S(1)} %get-tuple-element.6), channel_id=1, replica_groups=mesh['dp'=64,'mp'=4] {'mp'}, use_global_device_ids=true, to_apply=%region_11.12 | all-reduce | flops 128 | bytes 1024 | tf_op jit(solution)/shard_map/psum | solution.py:105
  600.9 0.8 fusion.29
  (38 shorter events, 0.6 us)
Async XLA Ops:
  7.2 82.8 %copy-start = (bf16[128,512]{1,0:T(8,128)(2,1)S(1)}, bf16[128,512]{1,0:T(8,128)(2,1)}, u32[]{:S(2)}) copy-start(bf16[128,512]{1,0:T(8,128)(2,1)} %param.14) | copy-start | bytes 393220
  7.2 82.8 %all-gather.11.cloned.1.call-start = ((), (), s32[]{:S(2)}) async-start(), calls=%async_computation.4 | async-start | bytes 2129920 | tf_op jit(solution)/shard_map/all_gather | solution.py:37
  7.9 110.3 %reduce-scatter.3.cloned.1.call-start = ((), (), s32[]{:S(2)}) async-start(), calls=%async_computation.5 | async-start | bytes 1310720 | tf_op jit(solution)/shard_map/reduce_scatter | solution.py:38
  93.3 3.3 copy-start.3
  93.4 5.8 copy-start.7
  93.4 24.9 %copy-start.2 = (bf16[128,512]{1,0:T(8,128)(2,1)S(1)}, bf16[128,512]{1,0:T(8,128)(2,1)}, u32[]{:S(2)}) copy-start(bf16[128,512]{1,0:T(8,128)(2,1)} %param.15) | copy-start | bytes 393220
  93.4 34.4 %copy-start.5 = (f32[512]{0:T(512)S(1)}, f32[512]{0:T(512)}, u32[]{:S(2)}) copy-start(f32[512]{0:T(512)} %param.17) | copy-start | bytes 6148
  93.4 110.0 %all-gather.19.cloned.1.call-start = ((), (), s32[]{:S(2)}) async-start(), calls=%async_computation.10 | async-start | bytes 7208960 | tf_op jit(solution)/shard_map/all_gather | solution.py:81
  94.1 156.8 %all-gather.21.cloned.1.call-start = ((), (), s32[]{:S(2)}) async-start(), calls=%async_computation.11 | async-start | bytes 7208960 | tf_op jit(solution)/shard_map/all_gather | solution.py:82
  94.7 222.5 %all-gather.23.cloned.1.call-start = ((), (), s32[]{:S(2)}) async-start(), calls=%async_computation.12 | async-start | bytes 7208960 | tf_op jit(solution)/shard_map/all_gather | solution.py:87
  95.3 306.1 %all-gather.13.cloned.1.call-start = ((), (), s32[]{:S(2)}) async-start(), calls=%async_computation.6 | async-start | bytes 3194880 | tf_op jit(solution)/shard_map/all_gather | solution.py:47
  95.9 384.4 %all-gather.15.cloned.1.call-start = ((), (), s32[]{:S(2)}) async-start(), calls=%async_computation.7 | async-start | bytes 3194880 | tf_op jit(solution)/shard_map/all_gather | solution.py:48
  163.8 39.4 %all-to-all-start = ((bf16[64,4,2048]{2,1,0:T(4,128)(2,1)}), bf16[64,4,2048]{2,1,0:T(4,128)(2,1)S(1)}, u32[]{:S(2)}, u32[]{:S(2)}) async-start(bf16[64,4,2048]{2,1,0:T(4,128)(2,1)} %reshape.214), calls=%async_computation.1 | async-start | bytes 2097152 | tf_op jit(solution)/shard_map/all_to_all | solution.py:72
  174.3 384.9 %all-gather.17.cloned.1.call-start = ((), (), s32[]{:S(2)}) async-start(), calls=%async_computation.8 | async-start | bytes 3194880 | tf_op jit(solution)/shard_map/all_gather | solution.py:53
  325.5 12.3 %copy-start.4 = (f32[128,6]{0,1:T(8,128)S(1)}, f32[128,6]{0,1:T(8,128)}, u32[]{:S(2)}) copy-start(f32[128,6]{0,1:T(8,128)} %param.25) | copy-start | bytes 9220
  326.8 77.8 %all-to-all-start.1 = ((bf16[64,4,2048]{2,1,0:T(4,128)(2,1)}), bf16[64,4,2048]{2,1,0:T(4,128)(2,1)S(1)}, u32[]{:S(2)}, u32[]{:S(2)}) async-start(bf16[64,4,2048]{2,1,0:T(4,128)(2,1)} %reshape.216), calls=%async_computation.2 | async-start | bytes 2097152 | tf_op jit(solution)/shard_map/all_to_all | solution.py:90
  337.3 254.0 %reduce-scatter.5.cloned.1.call-start = ((), (), s32[]{:S(2)}) async-start(), calls=%async_computation.9 | async-start | bytes 1310720 | tf_op jit(solution)/shard_map/reduce_scatter | solution.py:102
  422.3 178.6 %copy-start.6 = (f32[512]{0:T(512)S(1)}, f32[512]{0:T(512)}, u32[]{:S(2)}) copy-start(f32[512]{0:T(512)} %param.27) | copy-start | bytes 6148
  592.4 9.3 %copy-start.1 = (bf16[128,512]{1,0:T(8,128)(2,1)}, bf16[128,512]{1,0:T(8,128)(2,1)S(1)}, u32[]{:S(2)}) copy-start(bf16[128,512]{1,0:T(8,128)(2,1)S(1)} %get-tuple-element.7) | copy-start | bytes 393220
Sparse Core Ops, SparseCore 0:
  10.8 79.1 all-gather.10
  93.5 24.6 reduce-scatter.2
  120.2 64.3 all-gather.18
  186.4 64.4 all-gather.20
  252.7 64.4 all-gather.22
  320.2 81.0 all-gather.12
  404.5 75.7 all-gather.14
  483.4 75.7 all-gather.16
  566.6 24.7 reduce-scatter.4
where the time goes:
time: 609 us; the launch traced here: 608 us
  waiting for transfers between devices  467 us (77%)
  local copies, waits for them, and re-layouts  35.3 us (6%)
  blocking collectives  31.2 us (5%)
  matrix products  27.6 us (5%)
  starting transfers between devices  21.7 us (4%)
  between operations  14.1 us (2%)
  other arithmetic  11.7 us (2%)
    all_gather x1, waiting for transfers between devices, local(): lax.all_gather(out_weight, 'dp', axis=1, tiled=True)  82 us
    all_gather x1, waiting for transfers between devices, local(): lax.all_gather(shared_down, 'dp', axis=1, tiled=True)  78.9 us
    all_gather x1, waiting for transfers between devices, local(): lax.all_gather(down_local, 'mp', axis=0, tiled=True)  66.3 us
    all_gather x1, waiting for transfers between devices, local(): lax.all_gather(shared_gate, 'dp', axis=0, tiled=True)  63.4 us
    all_gather x1, waiting for transfers between devices, local(): lax.all_gather(shared_up, 'dp', axis=0, tiled=True)  58 us
    all_gather x1, waiting for transfers between devices, local(): lax.all_gather(up_local, 'mp', axis=1, tiled=True)  41.9 us
    all_to_all x1, waiting for transfers between devices, local(): lax.all_to_all(outgoing.reshape(experts, quarter, model_width), 'dp', spl...  28 us
    dot_general x5, matrix products, matmul(): return jnp.dot(left, right, preferred_element_type=jnp.float32)  27.6 us
  transfers between devices with their start and end apart: 11, of which 9 were waited for; matrix products, arithmetic and copies ran while one was open for 10% of the time, Pallas kernels for 0%

commit v1 on v0

--- a/solution.py
+++ b/solution.py
@@ -34,7 +34,12 @@
     experts = lax.axis_size("dp")
     capacity = min(tok_rows, 8 * tok_rows // experts)
     model_width = D
-    partial_value = matmul(attention, lax.all_gather(out_weight, "dp", axis=1, tiled=True))
+    partial_value = matmul(
+        attention,
+        jnp.concatenate(
+            lax.all_to_all(jnp.stack([out_weight] * lax.axis_size("dp")), "dp", 0, 0), axis=1
+        ),
+    )
     projected = lax.psum_scatter(partial_value, "mp", scatter_dimension=1, tiled=True)
     hidden = (residual.astype(jnp.float32) + projected).astype(jnp.bfloat16)
     hidden_float = hidden.astype(jnp.float32)

time: 609 us -> 586 us (0.962)
  waiting for transfers between devices: 467 us -> 381 us
  blocking collectives: 31.2 us -> 94.8 us
    all_gather x1 -> x0, waiting for transfers between devices: 82 us -> none  [local(): lax.all_gather(out_weight, 'dp', axis=1, tiled=True)]
    all_to_all x0 -> x1, blocking collectives: none -> 63.2 us  [local(): lax.all_to_all(jnp.stack([out_weight] * lax.axis_size('dp')), 'dp', 0, 0)]
  transfers between devices with their start and end apart: 11 -> 10, of which waited for: 9 -> 8; matrix products, arithmetic and copies ran while one was open for 10% -> 11% of each run, Pallas kernels for 0% -> 0%
where the time goes in v1:
time: 586 us
  waiting for transfers between devices  381 us (65%)
  blocking collectives  94.8 us (16%)
  local copies, waits for them, and re-layouts  36.4 us (6%)
  matrix products  26 us (4%)
  starting transfers between devices  21.7 us (4%)
  between operations  14.4 us (2%)
  other arithmetic  11.7 us (2%)
    all_gather x1, waiting for transfers between devices, local(): lax.all_gather(shared_down, 'dp', axis=1, tiled=True)  78.9 us
    all_gather x1, waiting for transfers between devices, local(): lax.all_gather(down_local, 'mp', axis=0, tiled=True)  66.3 us
    all_gather x1, waiting for transfers between devices, local(): lax.all_gather(shared_gate, 'dp', axis=0, tiled=True)  63.2 us
    all_to_all x1, blocking collectives, local(): lax.all_to_all(jnp.stack([out_weight] * lax.axis_size('dp')), 'dp', 0, 0)  63.2 us
    all_gather x1, waiting for transfers between devices, local(): lax.all_gather(shared_up, 'dp', axis=0, tiled=True)  57.8 us
    all_gather x1, waiting for transfers between devices, local(): lax.all_gather(up_local, 'mp', axis=1, tiled=True)  41.6 us
    all_to_all x1, waiting for transfers between devices, local(): lax.all_to_all(outgoing.reshape(experts, quarter, model_width), 'dp', spl...  28 us
    dot_general x5, matrix products, matmul(): return jnp.dot(left, right, preferred_element_type=jnp.float32)  26 us
  transfers between devices with their start and end apart: 10, of which 8 were waited for; matrix products, arithmetic and copies ran while one was open for 11% of the time, Pallas kernels for 0%

profile of v1, /device:TPU:8, one launch (start us, length us, event | category | flops | bytes accessed | tf_op | source)
XLA Modules:
  0.0 585.8 jit_solution(5083724393605672194)
XLA Ops:
  7.2 1.0 stack.2
  8.3 63.2 %all_to_all.15 = bf16[64,512,32]{1,2,0:T(8,128)(2,1)S(1)} all-to-all(bf16[64,512,32]{1,2,0:T(8,128)(2,1)S(1)} %stack.2), channel_id=1, replica_groups=mesh['dp'=64,'mp'=4] {'dp'}, dimensions={0} | all-to-all | bytes 4194304 | tf_op jit(solution)/shard_map/all_to_all | solution.py:40
  71.4 1.8 fusion.50
  73.3 0.7 all-gather.16.cloned.1.call-update
  74.0 0.7 all-gather.18.cloned.1.call-update
  74.8 0.5 all-gather.20.cloned.1.call-update
  75.3 0.5 all-gather.10.cloned.1.call-update
  75.9 0.5 all-gather.12.cloned.1.call-update
  76.5 0.1 copy.25
  76.6 0.1 eq.55
  76.7 0.1 eq.51
  76.9 1.8 reduce-window.6
  78.7 0.3 slice_reduce_fusion
  79.0 0.1 fusion.36
  79.3 16.3 %reduce-scatter.3.cloned.1.call-done = f32[128,512]{1,0:T(8,128)} async-done(((f32[128,2048]{1,0:T(8,128)}), f32[128,512]{1,0:T(8,128)}) %reduce-scatter.3.cloned.1.call-update) | async-done | bytes 262160 | tf_op jit(solution)/shard_map/reduce_scatter | solution.py:43
  95.6 1.1 fusion.30
  96.7 8.5 %psum.14 = f32[128]{0:T(128)S(1)} all-reduce(f32[128]{0:T(128)S(1)} %get-tuple-element.8), channel_id=1, replica_groups=mesh['dp'=64,'mp'=4] {'mp'}, use_global_device_ids=true, to_apply=%region_6.7 | all-reduce | flops 128 | bytes 1024 | tf_op jit(solution)/shard_map/psum | solution.py:46
  105.2 0.1 fusion.32
  105.3 14.6 %all_gather.21 = bf16[128,2048]{1,0:T(8,128)(2,1)S(1)} all-gather(bf16[128,512]{1,0:T(8,128)(2,1)S(1)} %fusion.32), channel_id=1, replica_groups=mesh['dp'=64,'mp'=4] {'mp'}, dimensions={1}, use_global_device_ids=true | all-gather | bytes 655360 | tf_op jit(solution)/shard_map/all_gather | solution.py:50
  119.9 20.4 %scatter_custom_fusion = bf16[256,2048]{1,0:T(8,128)(2,1)S(1)} fusion(s32[768]{0:T(1024)S(1)} %get-tuple-element.5, bf16[128,2048]{1,0:T(8,128)(2,1)S(1)} %all_gather.21, s32[1024]{0:T(1024)S(1)} %pad_clamp_fusion.1, bf16[]{:T(256)} %constant.52.clone.1), kind=kCustom, calls=%fused_computation.10 | custom fusion | bytes 1048578 | tf_op jit(solution)/shard_map/scatter | solution.py:75
  140.3 1.3 reshape.224
  141.6 10.6 %all-to-all-start.1 = ((bf16[64,4,2048]{2,1,0:T(4,128)(2,1)}), bf16[64,4,2048]{2,1,0:T(4,128)(2,1)S(1)}, u32[]{:S(2)}, u32[]{:S(2)}) async-start(bf16[64,4,2048]{2,1,0:T(4,128)(2,1)} %reshape.224), calls=%async_computation.2 | async-start | bytes 2097152 | tf_op jit(solution)/shard_map/all_to_all | solution.py:77
  152.2 0.7 all-gather.14.cloned.1.call-update
  152.9 28.0 %all-to-all-done.1 = bf16[64,4,2048]{2,1,0:T(4,128)(2,1)S(1)} async-done(((bf16[64,4,2048]{2,1,0:T(4,128)(2,1)}), bf16[64,4,2048]{2,1,0:T(4,128)(2,1)S(1)}, u32[]{:S(2)}, u32[]{:S(2)}) %all-to-all-start.1) | async-done | bytes 1048608 | tf_op jit(solution)/shard_map/all_to_all | solution.py:77
  181.0 0.3 reshape.225
  181.3 5.6 fusion.4
  186.8 41.6 %all-gather.18.cloned.1.call-done = bf16[1,2048,1408]{1,2,0:T(8,128)(2,1)} async-done(((bf16[1,2048,352]{1,2,0:T(8,128)(2,1)}), bf16[1,2048,1408]{1,2,0:T(8,128)(2,1)}) %all-gather.18.cloned.1.call-update) | async-done | bytes 5767184 | tf_op jit(solution)/shard_map/all_gather | solution.py:87
  228.5 66.3 %all-gather.20.cloned.1.call-done = bf16[1,1408,2048]{2,1,0:T(8,128)(2,1)} async-done(((bf16[1,352,2048]{2,1,0:T(8,128)(2,1)}), bf16[1,1408,2048]{2,1,0:T(8,128)(2,1)}) %all-gather.20.cloned.1.call-update) | async-done | bytes 5767184 | tf_op jit(solution)/shard_map/all_gather | solution.py:92
  294.8 8.3 %fusion.14 = bf16[256,2048]{1,0:T(8,128)(2,1)S(1)} fusion(bf16[1,1408,2048]{2,1,0:T(8,128)(2,1)} %all-gather.20.cloned.1.call-done, bf16[256,2048]{1,0:T(8,128)(2,1)S(1)} %reshape.225, bf16[1,2048,1408]{1,2,0:T(8,128)(2,1)} %all-gather.18.cloned.1.call-done, f32[256,1408]{1,0:T(8,128)} %fusion.4), kind=kOutput, calls=%fused_computation.14 | convolution fusion | flops 2955476992 | bytes 15073280 | tf_op jit(solution)/shard_map/dot_general | solution.py:11
  303.1 1.2 reshape.226
  304.3 10.6 %all-to-all-start.2 = ((bf16[64,4,2048]{2,1,0:T(4,128)(2,1)}), bf16[64,4,2048]{2,1,0:T(4,128)(2,1)S(1)}, u32[]{:S(2)}, u32[]{:S(2)}) async-start(bf16[64,4,2048]{2,1,0:T(4,128)(2,1)} %reshape.226), calls=%async_computation.3 | async-start | bytes 2097152 | tf_op jit(solution)/shard_map/all_to_all | solution.py:95
  314.9 0.3 reduce-scatter.5.cloned.1.call-start
  315.2 0.1 reduce_sum.53
  315.3 0.1 copy.28
  315.4 0.1 copy.32
  315.5 63.2 %all-gather.10.cloned.1.call-done = bf16[2048,704]{1,0:T(8,128)(2,1)} async-done(((bf16[32,704]{1,0:T(8,128)(2,1)}), bf16[2048,704]{1,0:T(8,128)(2,1)}) %all-gather.10.cloned.1.call-update) | async-done | bytes 2883600 | tf_op jit(solution)/shard_map/all_gather | solution.py:52
  378.7 3.2 fusion.51
  381.9 0.3 reshape.227
  382.2 4.3 gather_fusion
  386.6 6.6 %reshape.228 = f32[128,6,2048]{2,1,0:T(8,128)} reshape(bf16[768,2048]{1,0:T(8,128)(2,1)} %gather_fusion) | data formatting | bytes 9437184 | tf_op jit(solution)/shard_map/convert_element_type | solution.py:105
  393.1 6.6 %multiply_reduce_fusion = f32[128,2048]{1,0:T(8,128)S(1)} fusion(f32[128,6,2048]{2,1,0:T(8,128)} %reshape.228, f32[128,6]{1,0:T(8,128)S(1)} %copy.32), kind=kLoop, calls=%fused_computation.3 | loop fusion | flops 2883584 | bytes 7343104 | tf_op jit(solution)/shard_map/reduce_sum | solution.py:106
  399.7 57.8 %all-gather.12.cloned.1.call-done = bf16[2048,704]{1,0:T(8,128)(2,1)} async-done(((bf16[32,704]{1,0:T(8,128)(2,1)}), bf16[2048,704]{1,0:T(8,128)(2,1)}) %all-gather.12.cloned.1.call-update) | async-done | bytes 2883600 | tf_op jit(solution)/shard_map/all_gather | solution.py:53
  457.5 78.9 %all-gather.14.cloned.1.call-done = bf16[704,2048]{0,1:T(8,128)(2,1)} async-done(((bf16[704,32]{0,1:T(8,128)(2,1)}), bf16[704,2048]{0,1:T(8,128)(2,1)}) %all-gather.14.cloned.1.call-update) | async-done | bytes 2883600 | tf_op jit(solution)/shard_map/all_gather | solution.py:58
  536.5 7.2 %convolution_add_fusion = f32[128,2048]{1,0:T(8,128)} fusion(f32[128,2048]{1,0:T(8,128)S(1)} %multiply_reduce_fusion, bf16[704,2048]{0,1:T(8,128)(2,1)} %all-gather.14.cloned.1.call-done, bf16[128,2048]{1,0:T(8,128)(2,1)S(1)} %all_gather.21, bf16[2048,704]{1,0:T(8,128)(2,1)} %all-gather.12.cloned.1.call-done, f32[128,704]{0,1:T(8,128)S(1)} %fusion.51), kind=kOutput, calls=%fused_computation.15 | convolution fusion | flops 739000320 | bytes 8749056 | tf_op jit(solution)/shard_map/dot_general | solution.py:11
  543.7 24.9 %reduce-scatter.5.cloned.1.call-done = f32[128,512]{1,0:T(8,128)} async-done(((f32[128,2048]{1,0:T(8,128)}), f32[128,512]{1,0:T(8,128)}) %reduce-scatter.5.cloned.1.call-update) | async-done | bytes 262160 | tf_op jit(solution)/shard_map/reduce_scatter | solution.py:107
  568.6 1.1 fusion.27
  569.7 8.5 %psum.15 = f32[128]{0:T(128)S(1)} all-reduce(f32[128]{0:T(128)S(1)} %get-tuple-element.6), channel_id=1, replica_groups=mesh['dp'=64,'mp'=4] {'mp'}, use_global_device_ids=true, to_apply=%region_11.12 | all-reduce | flops 128 | bytes 1024 | tf_op jit(solution)/shard_map/psum | solution.py:110
  578.2 0.8 fusion.29
  (37 shorter events, 0.6 us)
Async XLA Ops:
  7.2 64.3 %copy-start = (bf16[128,512]{1,0:T(8,128)(2,1)S(1)}, bf16[128,512]{1,0:T(8,128)(2,1)}, u32[]{:S(2)}) copy-start(bf16[128,512]{1,0:T(8,128)(2,1)} %param.14) | copy-start | bytes 393220
  7.2 88.4 %reduce-scatter.3.cloned.1.call-start = ((), (), s32[]{:S(2)}) async-start(), calls=%async_computation.5 | async-start | bytes 1310720 | tf_op jit(solution)/shard_map/reduce_scatter | solution.py:43
  73.2 3.3 copy-start.3
  73.2 5.8 copy-start.7
  73.2 22.4 %copy-start.2 = (bf16[128,512]{1,0:T(8,128)(2,1)S(1)}, bf16[128,512]{1,0:T(8,128)(2,1)}, u32[]{:S(2)}) copy-start(bf16[128,512]{1,0:T(8,128)(2,1)} %param.15) | copy-start | bytes 393220
  73.2 32.0 %copy-start.5 = (f32[512]{0:T(512)S(1)}, f32[512]{0:T(512)}, u32[]{:S(2)}) copy-start(f32[512]{0:T(512)} %param.17) | copy-start | bytes 6148
  73.2 108.0 %all-gather.16.cloned.1.call-start = ((), (), s32[]{:S(2)}) async-start(), calls=%async_computation.10 | async-start | bytes 7208960 | tf_op jit(solution)/shard_map/all_gather | solution.py:86
  74.0 154.5 %all-gather.18.cloned.1.call-start = ((), (), s32[]{:S(2)}) async-start(), calls=%async_computation.11 | async-start | bytes 7208960 | tf_op jit(solution)/shard_map/all_gather | solution.py:87
  74.7 220.1 %all-gather.20.cloned.1.call-start = ((), (), s32[]{:S(2)}) async-start(), calls=%async_computation.12 | async-start | bytes 7208960 | tf_op jit(solution)/shard_map/all_gather | solution.py:92
  75.3 303.4 %all-gather.10.cloned.1.call-start = ((), (), s32[]{:S(2)}) async-start(), calls=%async_computation.6 | async-start | bytes 3194880 | tf_op jit(solution)/shard_map/all_gather | solution.py:52
  75.9 381.6 %all-gather.12.cloned.1.call-start = ((), (), s32[]{:S(2)}) async-start(), calls=%async_computation.7 | async-start | bytes 3194880 | tf_op jit(solution)/shard_map/all_gather | solution.py:53
  141.6 39.4 %all-to-all-start.1 = ((bf16[64,4,2048]{2,1,0:T(4,128)(2,1)}), bf16[64,4,2048]{2,1,0:T(4,128)(2,1)S(1)}, u32[]{:S(2)}, u32[]{:S(2)}) async-start(bf16[64,4,2048]{2,1,0:T(4,128)(2,1)} %reshape.224), calls=%async_computation.2 | async-start | bytes 2097152 | tf_op jit(solution)/shard_map/all_to_all | solution.py:77
  152.2 384.3 %all-gather.14.cloned.1.call-start = ((), (), s32[]{:S(2)}) async-start(), calls=%async_computation.8 | async-start | bytes 3194880 | tf_op jit(solution)/shard_map/all_gather | solution.py:58
  303.1 12.3 %copy-start.4 = (f32[128,6]{0,1:T(8,128)S(1)}, f32[128,6]{0,1:T(8,128)}, u32[]{:S(2)}) copy-start(f32[128,6]{0,1:T(8,128)} %param.25) | copy-start | bytes 9220
  304.3 77.6 %all-to-all-start.2 = ((bf16[64,4,2048]{2,1,0:T(4,128)(2,1)}), bf16[64,4,2048]{2,1,0:T(4,128)(2,1)S(1)}, u32[]{:S(2)}, u32[]{:S(2)}) async-start(bf16[64,4,2048]{2,1,0:T(4,128)(2,1)} %reshape.226), calls=%async_computation.3 | async-start | bytes 2097152 | tf_op jit(solution)/shard_map/all_to_all | solution.py:95
  314.9 253.7 %reduce-scatter.5.cloned.1.call-start = ((), (), s32[]{:S(2)}) async-start(), calls=%async_computation.9 | async-start | bytes 1310720 | tf_op jit(solution)/shard_map/reduce_scatter | solution.py:107
  399.7 178.5 %copy-start.6 = (f32[512]{0:T(512)S(1)}, f32[512]{0:T(512)}, u32[]{:S(2)}) copy-start(f32[512]{0:T(512)} %param.27) | copy-start | bytes 6148
  569.6 9.3 %copy-start.1 = (bf16[128,512]{1,0:T(8,128)(2,1)}, bf16[128,512]{1,0:T(8,128)(2,1)S(1)}, u32[]{:S(2)}) copy-start(bf16[128,512]{1,0:T(8,128)(2,1)S(1)} %get-tuple-element.7) | copy-start | bytes 393220
Sparse Core Ops, SparseCore 0:
  73.3 22.2 reduce-scatter.2
  97.6 64.4 all-gather.15
  164.1 64.3 all-gather.17
  230.3 64.4 all-gather.19
  297.8 80.9 all-gather.9
  381.7 75.7 all-gather.11
  460.7 75.7 all-gather.13
  543.8 24.7 reduce-scatter.4
